TPU v7x, 32 devices: a whole 2x2x4 slice. The times are simulated.
32 devices in a mesh: rep: 2 (over y), sample: 4 (over z), head: 4 (over x, core).
Axes of the slice: x: 2, y: 2, z: 4, core: 2. Of those that a mesh axis runs over, the one named last changes fastest.
Arguments:
- x_pre: bfloat16 [8, 128, 8192], P(('rep', 'sample'), None, 'head'), parts along dimension 0, may hold values from -120 to 120
- z_pre: bfloat16 [8, 128, 8192], P(('rep', 'sample'), None, 'head'), parts along dimension 0, may hold values from -6 to 6
- b_pre: bfloat16 [8, 128, 512], P(('rep', 'sample')), parts along dimension 0, may hold values from -1.796875 to 1.796875
- c_pre: bfloat16 [8, 128, 512], P(('rep', 'sample')), parts along dimension 0, may hold values from -0.5390625 to 0.5390625
- dt_pre: float32 [8, 128, 128], P(('rep', 'sample'), None, 'head'), parts along dimension 0, may hold values from -1.5 to 7.5
- lengths: int32 [8], P(('rep', 'sample')), parts along dimension 0, may hold values from 64 to 128, as said below
- init_state: float32 [8, 128, 8192], P(('rep', 'sample'), None, 'head'), parts along dimension 0, may hold values from -6 to 6
- a_rates: float32 [128], P('head'), may hold values from 0.005 to 0.3
- dt_bias: float32 [128], P('head'), may hold values from -2 to -1
- skip_scale: float32 [128], P('head'), may hold values from 0.5 to 2
- norm_gain: float32 [8192], P('head'), may hold values from 0.5 to 1.5
- x_dec: bfloat16 [8, 4, 8192], P(('rep', 'sample'), None, 'head'), parts along dimension 0, may hold values from -120 to 120
- z_dec: bfloat16 [8, 4, 8192], P(('rep', 'sample'), None, 'head'), parts along dimension 0, may hold values from -6 to 6
- b_dec: bfloat16 [8, 4, 512], P(('rep', 'sample')), parts along dimension 0, may hold values from -6 to 6
- c_dec: bfloat16 [8, 4, 512], P(('rep', 'sample')), parts along dimension 0, may hold values from -0.5390625 to 0.5390625
- dt_dec: float32 [8, 4, 128], P(('rep', 'sample'), None, 'head'), parts along dimension 0, may hold values from -3 to 3
Outputs:
- out_pre: bfloat16 [8, 128, 8192], P(('rep', 'sample'), None, 'head'), parts along dimension 0
- final_state: bfloat16 [8, 128, 8192], P(('rep', 'sample'), None, 'head'), parts along dimension 0
- out_dec: bfloat16 [8, 4, 8192], P(('rep', 'sample'), None, 'head'), parts along dimension 0
There are 2 independent parts, one for each index of `rep`. A program takes and returns all parts, laid end to end along the dimension named above; an argument that names none is the same for every part. Nothing has to cross between parts.
Inputs may be any that keep to these rules, and one draw needn't show every extreme that they name: Each prompt's valid tokens are the first lengths[p] of its 128 positions; some prompt uses all 128.
All inputs are finite; a program needn't handle non-finite values.
Results may differ from a plain program's by a relative error of at most 0.006.
Values may be sent and summed in bfloat16 or wider, within the bound.
No kernel may reach another device: no remote copies, remote signals or barrier semaphores. Data moves between devices by JAX's collectives and lax.ppermute only.
A program may use at most 64 MiB of HBM per device.

v0:
```python
import jax
import jax.numpy as jnp
from jax import lax
from jax.sharding import PartitionSpec as P

H = 128
P_SIZE = 64
G = 4
BLOCK = 128
epsilon = 1e-05
highest = lax.Precision.HIGHEST


def group_owners(first_head, head_count):
    head_ids = first_head + jnp.arange(head_count, dtype=jnp.int32)
    return head_ids // (H // G)


def group_pick(owners):
    return (owners[:, None] == jnp.arange(G, dtype=jnp.int32)[None, :]).astype(jnp.float32)


def scan_prompt(inputs, b_rows, c_rows, step_delta, rates, skip_gain, start_state, owners):
    length = inputs.shape[0]
    head_count = step_delta.shape[1]
    head_width = inputs.shape[1] // head_count
    states = b_rows.shape[1] // G
    blocks = length // BLOCK
    b_groups = b_rows.reshape(blocks, BLOCK, G, states)
    c_groups = c_rows.reshape(blocks, BLOCK, G, states)
    group_scores = jnp.einsum(
        "cign,cjgn->cijg", c_groups, b_groups, preferred_element_type=jnp.float32
    )
    head_scores = jnp.take(group_scores, owners, axis=3)
    b_head = jnp.take(b_groups, owners, axis=2).astype(jnp.float32)
    c_head = jnp.take(c_groups, owners, axis=2).astype(jnp.float32)
    values = inputs.astype(jnp.float32).reshape(blocks, BLOCK, head_count, head_width)
    block_delta = step_delta.reshape(blocks, BLOCK, head_count)
    decays = jnp.cumsum(-block_delta * rates, axis=1)
    causal_mask = (jnp.arange(BLOCK)[:, None] >= jnp.arange(BLOCK)[None, :])[None, :, :, None]
    spread = decays[:, :, None, :] - decays[:, None, :, :]
    weights = jnp.where(causal_mask, jnp.exp(jnp.where(causal_mask, spread, 0.0)), 0.0)
    scores = head_scores * weights * block_delta[:, None, :, :]
    inner_part = jnp.einsum("cijh,cjhp->cihp", scores, values, precision=highest)
    tail_decay = jnp.exp(decays[:, -1:, :] - decays) * block_delta
    block_states = jnp.einsum(
        "cjhn,cjhp->cnhp", b_head * tail_decay[..., None], values, precision=highest
    )
    block_totals = jnp.exp(decays[:, -1, :])

    def carry_step(carried, pieces):
        factor, fresh_term = pieces
        return (factor[None, :, None] * carried + fresh_term, carried)

    final_carry, starts = lax.scan(
        carry_step,
        start_state.reshape(states, head_count, head_width),
        (block_totals, block_states),
    )
    outer_part = (
        jnp.einsum("cihn,cnhp->cihp", c_head, starts, precision=highest)
        * jnp.exp(decays)[..., None]
    )
    result = inner_part + outer_part + skip_gain[None, None, :, None] * values
    return (
        result.reshape(length, head_count * head_width),
        final_carry.reshape(states, head_count * head_width),
    )


def gate_values(result, gate_rows):
    gate_rows = gate_rows.astype(jnp.float32)
    return result * gate_rows * jax.nn.sigmoid(gate_rows)


def select_heads(c_rows, owners):
    shape_front = c_rows.shape[:2]
    states = c_rows.shape[2] // G
    grouped = c_rows.reshape(shape_front[0], shape_front[1], G, states)
    return jnp.take(grouped, owners, axis=2)


def body(
    x_pre,
    z_pre,
    b_pre,
    c_pre,
    dt_pre,
    lengths,
    init_state,
    a_rates,
    dt_bias,
    skip_scale,
    norm_gain,
    x_dec,
    z_dec,
    b_dec,
    c_dec,
    dt_dec,
):
    heads_here = a_rates.shape[0]
    head_width = x_pre.shape[2] // heads_here
    first_head = lax.axis_index("head") * heads_here
    owners = group_owners(first_head, heads_here)
    picker = group_pick(owners)
    length = x_pre.shape[1]
    positions = jnp.arange(length, dtype=jnp.int32)
    valid_mask = (positions[None, :] < lengths[:, None]).astype(jnp.float32)
    step_delta = jax.nn.softplus(dt_pre + dt_bias) * valid_mask[:, :, None]

    def one_prompt(pieces):
        inputs, b_rows, c_rows, prompt_delta, start_state = pieces
        return scan_prompt(
            inputs, b_rows, c_rows, prompt_delta, a_rates, skip_scale, start_state, owners
        )

    result, final_carry = lax.map(one_prompt, (x_pre, b_pre, c_pre, step_delta, init_state))
    final_state = final_carry.astype(jnp.bfloat16)
    gated_rows = gate_values(result, z_pre)
    pre_totals = lax.psum(jnp.sum(gated_rows * gated_rows, axis=-1), "head")
    norm_scale = lax.rsqrt(pre_totals[:, :, None] / (H * P_SIZE) + epsilon)
    out_pre = (gated_rows * norm_scale * norm_gain * valid_mask[:, :, None]).astype(jnp.bfloat16)
    slots_here = x_dec.shape[0]
    prompt_count = x_dec.shape[1]
    prompts_here = final_state.shape[0]
    states = final_state.shape[1]
    cached = final_state.reshape(prompts_here, states, heads_here, head_width)
    queries = lax.all_to_all(c_dec, "sample", split_axis=1, concat_axis=0, tiled=True)
    c_head = select_heads(queries, owners)
    answers = jnp.einsum("sphn,pnhq->sphq", c_head, cached, preferred_element_type=jnp.float32)
    answers = answers.reshape(answers.shape[0], prompts_here, heads_here * head_width)
    state_reads = lax.all_to_all(
        answers.astype(jnp.bfloat16), "sample", split_axis=0, concat_axis=1, tiled=True
    ).astype(answers.dtype)
    state_reads = state_reads.reshape(slots_here, prompt_count, heads_here, head_width)
    c_groups = c_dec.astype(jnp.float32).reshape(slots_here, prompt_count, G, states)
    b_groups = b_dec.astype(jnp.float32).reshape(slots_here, prompt_count, G, states)
    cb_dot = jnp.einsum("spgn,spgn->spg", c_groups, b_groups, precision=highest)
    cb_dot = jnp.einsum("spg,hg->sph", cb_dot, picker, precision=highest)
    step_sizes = jax.nn.softplus(dt_dec + dt_bias)
    decay_rate = jnp.exp(-step_sizes * a_rates)
    values = x_dec.astype(jnp.float32).reshape(slots_here, prompt_count, heads_here, head_width)
    fresh_term = (
        decay_rate[..., None] * state_reads + (step_sizes * cb_dot + skip_scale)[..., None] * values
    )
    gated_dec = gate_values(
        fresh_term.reshape(slots_here, prompt_count, heads_here * head_width), z_dec
    )
    dec_totals = lax.psum(jnp.sum(gated_dec * gated_dec, axis=-1), "head")
    dec_scale = lax.rsqrt(dec_totals[:, :, None] / (H * P_SIZE) + epsilon)
    out_dec = (gated_dec * dec_scale * norm_gain).astype(jnp.bfloat16)
    return (out_pre, final_state, out_dec)


def solution(mesh):
    in_specs = (
        P(("rep", "sample"), None, "head"),
        P(("rep", "sample"), None, "head"),
        P(("rep", "sample"), None, None),
        P(("rep", "sample"), None, None),
        P(("rep", "sample"), None, "head"),
        P(("rep", "sample")),
        P(("rep", "sample"), None, "head"),
        P("head"),
        P("head"),
        P("head"),
        P("head"),
        P(("rep", "sample"), None, "head"),
        P(("rep", "sample"), None, "head"),
        P(("rep", "sample"), None, None),
        P(("rep", "sample"), None, None),
        P(("rep", "sample"), None, "head"),
    )
    out_specs = (
        P(("rep", "sample"), None, "head"),
        P(("rep", "sample"), None, "head"),
        P(("rep", "sample"), None, "head"),
    )
    return jax.shard_map(body, mesh=mesh, in_specs=in_specs, out_specs=out_specs, check_vma=False)
```

profile of v0, /device:TPU:0, one launch (start us, length us, event | category | flops | bytes accessed | tf_op | source)
XLA Modules:
  0.0 61.4 jit_solution(16359119723385610459)
XLA Ops:
  0.7 0.8 %copy.168 = bf16[1,4,512]{2,0,1:T(2,128)(2,1)S(1)} copy(bf16[1,4,512]{2,1,0:T(4,128)(2,1)} %param.32) | data formatting | bytes 8192 | tf_op args[14]
  3.2 6.3 %all-to-all-start = ((bf16[4,2,256]{2,1,0:T(2,128)(2,1)}), bf16[4,2,256]{2,1,0:T(2,128)(2,1)}, u32[]{:S(2)}, u32[]{:S(2)}) async-start(bf16[4,2,256]{2,1,0:T(2,128)(2,1)} %reshape.510), calls=%async_computation | async-start | bytes 8192 | tf_op jit(solution)/shard_map/all_to_all | solution.py:128
  10.2 0.8 %negate_multiply_fusion = f32[1,128,32]{1,2,0:T(8,128)S(1)} fusion(f32[32]{0:T(128)} %param.25, f32[128]{0:T(128)S(1)} %compare_convert_fusion, f32[1,128,32]{1,2,0:T(8,128)} %param.22, f32[32]{0:T(128)} %param.26), kind=kLoop, calls=%fused_computation.73 | loop fusion | flops 40960 | bytes 33536 | tf_op jit(solution)/shard_map/while/body/eval_jaxpr/mul | solution.py:39
  13.2 0.9 %reshape.439 = bf16[128,4,128]{2,1,0:T(4,128)(2,1)S(1)} reshape(bf16[1,128,512]{2,1,0:T(8,128)(2,1)} %param.21) | data formatting | bytes 262144 | tf_op jit(solution)/shard_map/reshape.21
  14.1 1.0 %copy.129 = bf16[1,128,512]{1,2,0:T(8,128)(2,1)S(1)} copy(bf16[1,128,512]{2,1,0:T(8,128)(2,1)} %param.21) | data formatting | bytes 262144 | tf_op args[3]
  15.2 2.0 %copy.127 = bf16[1,128,2048]{1,2,0:T(8,128)(2,1)} copy(bf16[1,128,2048]{2,1,0:T(8,128)(2,1)} %param.18) | data formatting | bytes 1048576 | tf_op args[0]
  17.2 1.2 %copy.133 = f32[1,128,2048]{1,2,0:T(8,128)} copy(bf16[1,128,2048]{2,1,0:T(8,128)(2,1)S(1)} %copy-done.2) | data formatting | bytes 1572864 | tf_op jit(solution)/shard_map/while/body/eval_jaxpr/convert_element_type | solution.py:37
  18.4 0.8 %copy.136 = bf16[1,128,512]{1,2,0:T(8,128)(2,1)} copy(bf16[1,128,512]{2,1,0:T(8,128)(2,1)S(1)} %copy-done.6) | data formatting | bytes 262144 | tf_op args[2]
  20.3 0.7 %copy.125 = f32[128,32]{0,1:T(8,128)} copy(f32[128,32]{1,0:T(8,128)S(1)} %bitcast.135) | data formatting | bytes 32768 | tf_op jit(solution)/shard_map/while/body/eval_jaxpr/sub | solution.py:41
  22.8 0.7 %multiply_bitcast_fusion = (f32[128,32]{0,1:T(8,128)}, f32[128,32]{0,1:T(8,128)}) fusion(f32[1,128,32]{1,2,0:T(8,128)S(1)} %copy.138, f32[32]{0:T(128)S(1)} %slice_bitcast_fusion, f32[128]{0:T(128)S(1)} %compare_convert_fusion, f32[1,128,32]{1,2,0:T(8,128)S(1)} %copy-done.8, f32[32]{0:T(128)S(1)} %copy-done.18), kind=kLoop, calls=%fused_computation.72 | loop fusion | flops 40960 | bytes 66304 | tf_op jit(solution)/shard_map/while/body/eval_jaxpr/mul | solution.py:47
  23.7 0.8 %gather_fusion = f32[32,128,128]{1,2,0:T(8,128)S(1)} fusion(f32[128,128,4]{0,1,2:T(8,128)S(1)} %convolution_bitcast_fusion.1, s32[1024]{0:T(1024)} %pad_clamp_fusion.1), kind=kCustom, calls=%fused_computation.2 | custom fusion | bytes 4194432 | tf_op jit(solution)/shard_map/while/body/eval_jaxpr/jit(_take)/gather | solution.py:34
  24.5 1.9 %gather_fusion.2 = bf16[32,128,128]{2,1,0:T(8,128)(2,1)} fusion(bf16[128,4,128]{2,0,1:T(8,128)(2,1)S(1)} %bitcast.129, s32[1024]{0:T(1024)} %pad_clamp_fusion), kind=kCustom, calls=%fused_computation.clone | custom fusion | bytes 2097280 | tf_op jit(solution)/shard_map/while/body/eval_jaxpr/jit(_take)/gather | solution.py:36
  26.5 4.0 %fusion.12 = f32[1,128,32,64]{1,3,2,0:T(8,128)S(1)} fusion(bf16[128,32,64]{0,2,1:T(8,128)(2,1)} %bitcast.137, f32[32,128,128]{1,2,0:T(8,128)S(1)} %gather_fusion, f32[128,32]{0,1:T(8,128)S(1)} %copy-done.17, f32[128,32]{0,1:T(8,128)S(1)} %copy-done.12, pred[32]{0:T(512)(128)(4,1)S(1)} %copy-done.26, pred[128,128]{0,1:T(8,128)(4,1)S(1)} %copy-done.14), kind=kOutput, calls=%fused_computation.16 | convolution fusion | flops 405798912 | bytes 3719200 | tf_op jit(solution)/shard_map/while/body/eval_jaxpr/cijh,cjhp->cihp/dot_general | solution.py:44
  30.5 2.2 %fusion.17 = f32[1,128,32,64]{1,3,2,0:T(8,128)S(1)} fusion(f32[1,128,32,64]{1,3,2,0:T(8,128)S(1)} %fusion.12, f32[128,32,64]{0,2,1:T(8,128)S(1)} %bitcast.131, bf16[32,128,128]{2,1,0:T(8,128)(2,1)S(1)} %copy-done, f32[1,128,32,64]{1,3,2,0:T(8,128)S(1)} %bitcast.132, pred[32]{0:T(512)(128)(4,1)S(1)} %copy-done.26, f32[32]{0:T(128)S(1)} %copy-done.25, ...), kind=kOutput, calls=%fused_computation.20 | convolution fusion | flops 404226048 | bytes 5259424 | tf_op jit(solution)/shard_map/while/body/eval_jaxpr/cihn,cnhp->cihp/dot_general | solution.py:61
  33.8 1.8 %gather_fusion.3 = bf16[32,128,128]{2,1,0:T(8,128)(2,1)} fusion(bf16[128,4,128]{2,0,1:T(8,128)(2,1)S(1)} %bitcast.130, s32[1024]{0:T(1024)} %pad_clamp_fusion), kind=kCustom, calls=%fused_computation.1.clone | custom fusion | bytes 2097280 | tf_op jit(solution)/shard_map/while/body/eval_jaxpr/jit(_take)/gather | solution.py:35
  36.2 2.7 %fusion = f32[32,128,64]{1,2,0:T(8,128)S(1)} fusion(bf16[128,32,64]{0,2,1:T(8,128)(2,1)S(1)} %bitcast.138, bf16[32,128,128]{2,1,0:T(8,128)(2,1)} %gather_fusion.3, f32[128,32]{0,1:T(8,128)S(1)} %copy-done.16, pred[32]{0:T(512)(128)(4,1)S(1)} %copy-done.27), kind=kOutput, calls=%fused_computation.4 | convolution fusion | flops 404226048 | bytes 2637856 | tf_op jit(solution)/shard_map/while/body/eval_jaxpr/cjhn,cjhp->cnhp/dot_general | solution.py:46
  39.5 0.7 %reshape.511 = bf16[4,1,512]{2,1,0:T(2,128)(2,1)S(1)} reshape(bf16[4,2,256]{2,1,0:T(2,128)(2,1)} %all-to-all-done) | data formatting | bytes 8192
  40.2 0.7 %gather_fusion.1 = bf16[32,4,128]{2,1,0:T(4,128)(2,1)S(1)} fusion(bf16[4,4,128]{2,0,1:T(4,128)(2,1)S(1)} %bitcast.141, s32[1024]{0:T(1024)} %pad_clamp_fusion.1), kind=kCustom, calls=%fused_computation.3 | custom fusion | bytes 65664 | tf_op jit(solution)/shard_map/jit(_take)/gather | solution.py:80
  41.5 0.7 %reduce.7 = bf16[4,2048]{1,0:T(4,128)(2,1)S(1)} reduce(bf16[4,1,2048]{2,1,0:T(2,128)(2,1)S(1)} %convert_element_type.108, bf16[]{:T(256)} %broadcast.360), dimensions={1}, to_apply=%convert_element_type.108.reduce_sub_computation | reduce | bytes 32770 | tf_op jit(solution)/shard_map/convert_element_type | solution.py:133
  42.8 5.1 %all-to-all-start.1 = ((bf16[4,2,1024]{2,1,0:T(2,128)(2,1)}), bf16[4,2,1024]{2,1,0:T(2,128)(2,1)S(1)}, u32[]{:S(2)}, u32[]{:S(2)}) async-start(bf16[4,2,1024]{2,1,0:T(2,128)(2,1)} %reshape.512), calls=%async_computation.1 | async-start | bytes 32768 | tf_op jit(solution)/shard_map/all_to_all | solution.py:132
  48.1 1.0 %copy.145 = bf16[1,128,2048]{2,1,0:T(8,128)(2,1)} copy(bf16[1,128,2048]{1,2,0:T(8,128)(2,1)S(1)} %fusion.26) | data formatting | bytes 1048576
  49.5 4.0 %all-to-all-done.1 = bf16[4,2,1024]{2,1,0:T(2,128)(2,1)S(1)} async-done(((bf16[4,2,1024]{2,1,0:T(2,128)(2,1)}), bf16[4,2,1024]{2,1,0:T(2,128)(2,1)S(1)}, u32[]{:S(2)}, u32[]{:S(2)}) %all-to-all-start.1) | async-done | bytes 16416 | tf_op jit(solution)/shard_map/all_to_all | solution.py:132
  53.8 5.6 %all-reduce = (f32[1,128]{1,0:T(1,128)S(1)}, f32[1,4]{1,0:T(1,128)S(1)}) all-reduce(f32[1,128]{1,0:T(1,128)S(1)} %bitcast.143, f32[1,4]{1,0:T(1,128)S(1)} %bitcast.144), channel_id=1, replica_groups=mesh['rep'=2,'sample'=4,'head'=4] {'head'}, use_global_device_ids=true, to_apply=%region_2.4 | all-reduce | flops 132 | bytes 1056 | tf_op jit(solution)/shard_map/psum | solution.py:120
  60.2 1.2 %multiply_convert_fusion = bf16[1,128,2048]{2,1,0:T(8,128)(2,1)} fusion(f32[128]{0:T(128)S(1)} %copy-done.21, f32[2048]{0:T(1024)S(1)} %copy-done.9, f32[128]{0:T(128)S(1)} %rsqrt_bitcast_fusion.1, f32[1,128,2048]{2,1,0:T(8,128)S(1)} %copy.134, bf16[1,128,2048]{2,1,0:T(8,128)(2,1)S(1)} %copy-done.3), kind=kLoop, calls=%fused_computation.41 | loop fusion | flops 2621440 | bytes 2106368 | tf_op jit(solution)/shard_map/convert_element_type | solution.py:122
  (108 shorter events, 11.8 us)
Async XLA Ops:
  0.6 16.6 %copy-start.2 = (bf16[1,128,2048]{2,1,0:T(8,128)(2,1)S(1)}, bf16[1,128,2048]{2,1,0:T(8,128)(2,1)}, u32[]{:S(2)}) copy-start(bf16[1,128,2048]{2,1,0:T(8,128)(2,1)} %param.18) | copy-start | bytes 1572868
  0.6 17.8 %copy-start.6 = (bf16[1,128,512]{2,1,0:T(8,128)(2,1)S(1)}, bf16[1,128,512]{2,1,0:T(8,128)(2,1)}, u32[]{:S(2)}) copy-start(bf16[1,128,512]{2,1,0:T(8,128)(2,1)} %param.20) | copy-start | bytes 393220
  1.9 17.8 %copy-start.13 = (bf16[1,4,512]{2,1,0:T(4,128)(2,1)S(1)}, bf16[1,4,512]{2,1,0:T(4,128)(2,1)}, u32[]{:S(2)}) copy-start(bf16[1,4,512]{2,1,0:T(4,128)(2,1)} %param.32) | copy-start | bytes 12292
  3.2 36.3 %all-to-all-start = ((bf16[4,2,256]{2,1,0:T(2,128)(2,1)}), bf16[4,2,256]{2,1,0:T(2,128)(2,1)}, u32[]{:S(2)}, u32[]{:S(2)}) async-start(bf16[4,2,256]{2,1,0:T(2,128)(2,1)} %reshape.510), calls=%async_computation | async-start | bytes 8192 | tf_op jit(solution)/shard_map/all_to_all | solution.py:128
  10.2 12.5 %copy-start.20 = (f32[128]{0:T(128)}, f32[128]{0:T(128)S(1)}, u32[]{:S(2)}) copy-start(f32[128]{0:T(128)S(1)} %compare_convert_fusion) | copy-start | bytes 1540
  12.6 9.8 %copy-start.4 = (f32[1,128,2048]{2,1,0:T(8,128)S(1)}, f32[1,128,2048]{2,1,0:T(8,128)}, u32[]{:S(2)}) copy-start(f32[1,128,2048]{2,1,0:T(8,128)} %param.24) | copy-start | bytes 3145732
  17.2 5.6 %copy-start.8 = (f32[1,128,32]{1,2,0:T(8,128)S(1)}, f32[1,128,32]{1,2,0:T(8,128)}, u32[]{:S(2)}) copy-start(f32[1,128,32]{1,2,0:T(8,128)} %param.22) | copy-start | bytes 49156
  17.2 5.6 %copy-start.18 = (f32[32]{0:T(128)S(1)}, f32[32]{0:T(128)}, u32[]{:S(2)}) copy-start(f32[32]{0:T(128)} %param.26) | copy-start | bytes 388
  26.5 4.0 %copy-start = (bf16[32,128,128]{2,1,0:T(8,128)(2,1)S(1)}, bf16[32,128,128]{2,1,0:T(8,128)(2,1)}, u32[]{:S(2)}) copy-start(bf16[32,128,128]{2,1,0:T(8,128)(2,1)} %gather_fusion.2) | copy-start | bytes 3145732
  26.5 4.0 %copy-start.1 = (f32[1,128,2048]{1,2,0:T(8,128)S(1)}, f32[1,128,2048]{1,2,0:T(8,128)}, u32[]{:S(2)}) copy-start(f32[1,128,2048]{1,2,0:T(8,128)} %copy.133) | copy-start | bytes 3145732
  26.5 4.0 %copy-start.25 = (f32[32]{0:T(128)S(1)}, f32[32]{0:T(128)}, u32[]{:S(2)}) copy-start(f32[32]{0:T(128)} %param.27) | copy-start | bytes 388
  32.8 3.0 %copy-start.22 = (bf16[1,4,512]{2,1,0:T(4,128)(2,1)S(1)}, bf16[1,4,512]{2,1,0:T(4,128)(2,1)}, u32[]{:S(2)}) copy-start(bf16[1,4,512]{2,1,0:T(4,128)(2,1)} %param.31) | copy-start | bytes 12292
  32.8 3.0 %copy-start.19 = (f32[32]{0:T(128)S(1)}, f32[32]{0:T(128)}, u32[]{:S(2)}) copy-start(f32[32]{0:T(128)} %param.26) | copy-start | bytes 388
  32.8 3.0 %copy-start.23 = (f32[32]{0:T(128)S(1)}, f32[32]{0:T(128)}, u32[]{:S(2)}) copy-start(f32[32]{0:T(128)} %param.25) | copy-start | bytes 388
  33.2 3.0 %copy-start.5 = (bf16[1,128,2048]{1,2,0:T(8,128)(2,1)S(1)}, bf16[1,128,2048]{1,2,0:T(8,128)(2,1)}, u32[]{:S(2)}) copy-start(bf16[1,128,2048]{1,2,0:T(8,128)(2,1)} %copy.127) | copy-start | bytes 1572868
  33.2 3.0 %copy-start.16 = (f32[128,32]{0,1:T(8,128)S(1)}, f32[128,32]{0,1:T(8,128)}, u32[]{:S(2)}) copy-start(f32[128,32]{0,1:T(8,128)} %get-tuple-element.76) | copy-start | bytes 49156
  33.2 3.0 %copy-start.27 = (pred[32]{0:T(512)(128)(4,1)S(1)}, pred[32]{0:T(512)(128)(4,1)}, u32[]{:S(2)}) copy-start(pred[32]{0:T(512)(128)(4,1)} %compare_and_fusion) | copy-start | bytes 100
  36.2 3.2 %copy-start.15 = (bf16[4,4,128]{2,1,0:T(4,128)(2,1)S(1)}, bf16[4,4,128]{2,1,0:T(4,128)(2,1)}, u32[]{:S(2)}) copy-start(bf16[4,4,128]{2,1,0:T(4,128)(2,1)} %reshape.449) | copy-start | bytes 12292
  39.0 9.0 %copy-start.29 = (s32[32]{0:T(128)S(1)}, s32[32]{0:T(128)}, u32[]{:S(2)}) copy-start(s32[32]{0:T(128)} %get-tuple-element.79) | copy-start | bytes 388
  39.0 14.6 %copy-start.10 = (bf16[1,4,2048]{2,1,0:T(4,128)(2,1)S(1)}, bf16[1,4,2048]{2,1,0:T(4,128)(2,1)}, u32[]{:S(2)}) copy-start(bf16[1,4,2048]{2,1,0:T(4,128)(2,1)} %param.30) | copy-start | bytes 49156
  39.0 14.6 %copy-start.11 = (bf16[1,4,2048]{2,1,0:T(4,128)(2,1)S(1)}, bf16[1,4,2048]{2,1,0:T(4,128)(2,1)}, u32[]{:S(2)}) copy-start(bf16[1,4,2048]{2,1,0:T(4,128)(2,1)} %param.29) | copy-start | bytes 49156
  39.0 20.5 %copy-start.9 = (f32[2048]{0:T(1024)S(1)}, f32[2048]{0:T(1024)}, u32[]{:S(2)}) copy-start(f32[2048]{0:T(1024)} %param.28) | copy-start | bytes 24580
  39.0 21.2 %copy-start.21 = (f32[128]{0:T(128)S(1)}, f32[128]{0:T(128)}, u32[]{:S(2)}) copy-start(f32[128]{0:T(128)} %copy-done.20) | copy-start | bytes 1540
  42.8 10.7 %all-to-all-start.1 = ((bf16[4,2,1024]{2,1,0:T(2,128)(2,1)}), bf16[4,2,1024]{2,1,0:T(2,128)(2,1)S(1)}, u32[]{:S(2)}, u32[]{:S(2)}) async-start(bf16[4,2,1024]{2,1,0:T(2,128)(2,1)} %reshape.512), calls=%async_computation.1 | async-start | bytes 32768 | tf_op jit(solution)/shard_map/all_to_all | solution.py:132
  (8 other events, 17.2 us)
where the time goes:
time: 62.1 us; the launch traced here: 61.4 us
  local copies, waits for them, and re-layouts  20.3 us (33%)
  starting transfers between devices  11.4 us (18%)
  matrix products  9.71 us (16%)
  other arithmetic  8.5 us (14%)
  blocking collectives  5.63 us (9%)
  waiting for transfers between devices  4.02 us (6%)
  between operations  1.81 us (3%)
    unnamed x72, local copies, waits for them, and re-layouts  9.6 us
    all_to_all x1, starting transfers between devices, body(): lax.all_to_all(c_dec, 'sample', split_axis=1, concat_axis=0, tiled=True)  6.35 us
    psum x1, blocking collectives, body(): pre_totals = lax.psum(jnp.sum(gated_rows * gated_rows, axis=-1), 'head')  5.63 us
    all_to_all x1, starting transfers between devices, body(): lax.all_to_all(answers.astype(jnp.bfloat16), 'sample', split_axis=0, conc...  5.09 us
    all_to_all x1, waiting for transfers between devices, body(): lax.all_to_all(answers.astype(jnp.bfloat16), 'sample', split_axis=0, conc...  4.01 us
    dot_general x1, matrix products, scan_prompt(): jnp.einsum('cijh,cjhp->cihp', scores, values, precision=highest)  3.96 us
    dot_general x1, matrix products, scan_prompt(): jnp.einsum('cjhn,cjhp->cnhp', b_head * tail_decay[..., None], values, pre...  2.73 us
    dot_general x1, matrix products, scan_prompt(): jnp.einsum('cihn,cnhp->cihp', c_head, starts, precision=highest)  2.2 us
  transfers between devices with their start and end apart: 2, of which 1 were waited for; matrix products, arithmetic and copies ran while one was open for 49% of the time, Pallas kernels for 0%

commit v1 on v0

--- a/solution.py
+++ b/solution.py
@@ -117,7 +117,7 @@
     result, final_carry = lax.map(one_prompt, (x_pre, b_pre, c_pre, step_delta, init_state))
     final_state = final_carry.astype(jnp.bfloat16)
     gated_rows = gate_values(result, z_pre)
-    pre_totals = lax.psum(jnp.sum(gated_rows * gated_rows, axis=-1), "head")
+    pre_totals = jnp.sum(lax.all_gather(jnp.sum(gated_rows * gated_rows, axis=-1), "head"), axis=0)
     norm_scale = lax.rsqrt(pre_totals[:, :, None] / (H * P_SIZE) + epsilon)
     out_pre = (gated_rows * norm_scale * norm_gain * valid_mask[:, :, None]).astype(jnp.bfloat16)
     slots_here = x_dec.shape[0]

time: 62.1 us -> 66.8 us (1.076)
  blocking collectives: 5.63 us -> 10.7 us
  matrix products: 9.71 us -> 8.66 us
  other arithmetic: 8.5 us -> 9.48 us
    all_gather x0 -> x1, blocking collectives: none -> 5.06 us  [body(): lax.all_gather(jnp.sum(gated_rows * gated_rows, axis=-1), 'head')]
    reduce_sum x1 -> x2, other arithmetic: 0.41 us -> 1.51 us  [the longest x1 1.49 us: body(): jnp.sum(gated_rows * gated_rows, axis=-1)]
    dot_general x1, matrix products: 2.73 us -> 1.68 us  [scan_prompt(): jnp.einsum('cjhn,cjhp->cnhp', b_head * tail_decay[..., None], values, pre...]
  transfers between devices with their start and end apart: 2 -> 2, of which waited for: 1 -> 1; matrix products, arithmetic and copies ran while one was open for 49% -> 47% of each run, Pallas kernels for 0% -> 0%
where the time goes in v1:
time: 66.8 us; the launch traced here: 66.1 us
  local copies, waits for them, and re-layouts  20 us (30%)
  starting transfers between devices  11.4 us (17%)
  blocking collectives  10.7 us (16%)
  other arithmetic  9.48 us (14%)
  matrix products  8.66 us (13%)
  waiting for transfers between devices  4.02 us (6%)
  between operations  1.8 us (3%)
    unnamed x72, local copies, waits for them, and re-layouts  9.16 us
    all_to_all x1, starting transfers between devices, body(): lax.all_to_all(c_dec, 'sample', split_axis=1, concat_axis=0, tiled=True)  6.35 us
    psum x1, blocking collectives, body(): dec_totals = lax.psum(jnp.sum(gated_dec * gated_dec, axis=-1), 'head')  5.63 us
    all_to_all x1, starting transfers between devices, body(): lax.all_to_all(answers.astype(jnp.bfloat16), 'sample', split_axis=0, conc...  5.09 us
    all_gather x1, blocking collectives, body(): lax.all_gather(jnp.sum(gated_rows * gated_rows, axis=-1), 'head')  5.06 us
    all_to_all x1, waiting for transfers between devices, body(): lax.all_to_all(answers.astype(jnp.bfloat16), 'sample', split_axis=0, conc...  4.01 us
    dot_general x1, matrix products, scan_prompt(): jnp.einsum('cijh,cjhp->cihp', scores, values, precision=highest)  3.96 us
    dot_general x1, matrix products, scan_prompt(): jnp.einsum('cihn,cnhp->cihp', c_head, starts, precision=highest)  2.2 us
  transfers between devices with their start and end apart: 2, of which 1 were waited for; matrix products, arithmetic and copies ran while one was open for 47% of the time, Pallas kernels for 0%

profile of v1, /device:TPU:0, one launch (start us, length us, event | category | flops | bytes accessed | tf_op | source)
XLA Modules:
  0.0 66.1 jit_solution(13002857377517609837)
XLA Ops:
  0.7 0.8 %copy.168 = bf16[1,4,512]{2,0,1:T(2,128)(2,1)S(1)} copy(bf16[1,4,512]{2,1,0:T(4,128)(2,1)} %param.32) | data formatting | bytes 8192 | tf_op args[14]
  3.1 6.3 %all-to-all-start = ((bf16[4,2,256]{2,1,0:T(2,128)(2,1)}), bf16[4,2,256]{2,1,0:T(2,128)(2,1)}, u32[]{:S(2)}, u32[]{:S(2)}) async-start(bf16[4,2,256]{2,1,0:T(2,128)(2,1)} %reshape.511), calls=%async_computation | async-start | bytes 8192 | tf_op jit(solution)/shard_map/all_to_all | solution.py:128
  10.1 0.8 %negate_multiply_fusion = f32[1,128,32]{1,2,0:T(8,128)S(1)} fusion(f32[32]{0:T(128)} %param.25, f32[128]{0:T(128)S(1)} %compare_convert_fusion, f32[1,128,32]{1,2,0:T(8,128)} %param.22, f32[32]{0:T(128)} %param.26), kind=kLoop, calls=%fused_computation.73 | loop fusion | flops 40960 | bytes 33536 | tf_op jit(solution)/shard_map/while/body/eval_jaxpr/mul | solution.py:39
  13.1 0.9 %reshape.435 = bf16[128,4,128]{2,1,0:T(4,128)(2,1)S(1)} reshape(bf16[1,128,512]{2,1,0:T(8,128)(2,1)} %param.21) | data formatting | bytes 262144 | tf_op jit(solution)/shard_map/reshape.21
  14.0 1.0 %copy.129 = bf16[1,128,512]{1,2,0:T(8,128)(2,1)S(1)} copy(bf16[1,128,512]{2,1,0:T(8,128)(2,1)} %param.21) | data formatting | bytes 262144 | tf_op args[3]
  15.1 2.0 %copy.127 = bf16[1,128,2048]{1,2,0:T(8,128)(2,1)} copy(bf16[1,128,2048]{2,1,0:T(8,128)(2,1)} %param.18) | data formatting | bytes 1048576 | tf_op args[0]
  17.1 1.2 %copy.133 = f32[1,128,2048]{1,2,0:T(8,128)} copy(bf16[1,128,2048]{2,1,0:T(8,128)(2,1)S(1)} %copy-done.2) | data formatting | bytes 1572864 | tf_op jit(solution)/shard_map/while/body/eval_jaxpr/convert_element_type | solution.py:37
  18.3 0.8 %copy.136 = bf16[1,128,512]{1,2,0:T(8,128)(2,1)} copy(bf16[1,128,512]{2,1,0:T(8,128)(2,1)S(1)} %copy-done.7) | data formatting | bytes 262144 | tf_op args[2]
  22.7 0.7 %multiply_bitcast_fusion = (f32[128,32]{0,1:T(8,128)}, f32[128,32]{0,1:T(8,128)}) fusion(f32[1,128,32]{1,2,0:T(8,128)S(1)} %copy.138, f32[32]{0:T(128)S(1)} %slice_bitcast_fusion, f32[128]{0:T(128)S(1)} %compare_convert_fusion, f32[1,128,32]{1,2,0:T(8,128)S(1)} %copy-done.9, f32[32]{0:T(128)S(1)} %copy-done.19), kind=kLoop, calls=%fused_computation.72 | loop fusion | flops 40960 | bytes 66304 | tf_op jit(solution)/shard_map/while/body/eval_jaxpr/mul | solution.py:47
  23.7 0.8 %gather_fusion = f32[32,128,128]{1,2,0:T(8,128)S(1)} fusion(f32[128,128,4]{0,1,2:T(8,128)S(1)} %convolution_bitcast_fusion.1, s32[1024]{0:T(1024)} %pad_clamp_fusion.1), kind=kCustom, calls=%fused_computation.2 | custom fusion | bytes 4194432 | tf_op jit(solution)/shard_map/while/body/eval_jaxpr/jit(_take)/gather | solution.py:34
  24.5 2.0 %gather_fusion.2 = bf16[32,128,128]{2,1,0:T(8,128)(2,1)} fusion(bf16[128,4,128]{2,0,1:T(8,128)(2,1)S(1)} %bitcast.127, s32[1024]{0:T(1024)} %pad_clamp_fusion), kind=kCustom, calls=%fused_computation.clone | custom fusion | bytes 2097280 | tf_op jit(solution)/shard_map/while/body/eval_jaxpr/jit(_take)/gather | solution.py:36
  26.5 4.0 %fusion.12 = f32[1,128,32,64]{1,3,2,0:T(8,128)S(1)} fusion(bf16[128,32,64]{0,2,1:T(8,128)(2,1)} %bitcast.135, f32[32,128,128]{1,2,0:T(8,128)S(1)} %gather_fusion, f32[128,32]{0,1:T(8,128)S(1)} %copy-done.18, f32[128,32]{0,1:T(8,128)S(1)} %copy-done.13, pred[32]{0:T(512)(128)(4,1)S(1)} %copy-done.27, pred[128,128]{0,1:T(8,128)(4,1)S(1)} %copy-done.15), kind=kOutput, calls=%fused_computation.16 | convolution fusion | flops 405798912 | bytes 3719200 | tf_op jit(solution)/shard_map/while/body/eval_jaxpr/cijh,cjhp->cihp/dot_general | solution.py:44
  30.5 2.2 %fusion.17 = f32[1,128,32,64]{1,3,2,0:T(8,128)S(1)} fusion(f32[1,128,32,64]{1,3,2,0:T(8,128)S(1)} %fusion.12, f32[128,32,64]{0,2,1:T(8,128)S(1)} %bitcast.129, bf16[32,128,128]{2,1,0:T(8,128)(2,1)S(1)} %copy-done, f32[1,128,32,64]{1,3,2,0:T(8,128)S(1)} %bitcast.130, pred[32]{0:T(512)(128)(4,1)S(1)} %copy-done.27, f32[32]{0:T(128)S(1)} %copy-done.26, ...), kind=kOutput, calls=%fused_computation.20 | convolution fusion | flops 404226048 | bytes 5259424 | tf_op jit(solution)/shard_map/while/body/eval_jaxpr/cihn,cnhp->cihp/dot_general | solution.py:61
  33.2 1.5 %multiply_reduce_fusion = f32[128]{0:T(128)S(1)} fusion(f32[1,128,2048]{2,1,0:T(8,128)S(1)} %copy.134, bf16[1,128,2048]{2,1,0:T(8,128)(2,1)} %param.19), kind=kLoop, calls=%fused_computation.42 | loop fusion | flops 2097024 | bytes 1573376 | tf_op jit(solution)/shard_map/reduce_sum | solution.py:120
  34.7 5.1 %all-gather.1 = f32[4,1,128]{2,1,0:T(1,128)S(1)} all-gather(f32[1,1,128]{2,1,0:T(1,128)S(1)} %bitcast.141), channel_id=2, replica_groups=mesh['rep'=2,'sample'=4,'head'=4] {'head'}, dimensions={0}, use_global_device_ids=true | all-gather | bytes 2560 | tf_op jit(solution)/shard_map/all_gather | solution.py:120
  39.9 1.9 %gather_fusion.3 = bf16[32,128,128]{2,1,0:T(8,128)(2,1)} fusion(bf16[128,4,128]{2,0,1:T(8,128)(2,1)S(1)} %bitcast.128, s32[1024]{0:T(1024)} %pad_clamp_fusion), kind=kCustom, calls=%fused_computation.1.clone | custom fusion | bytes 2097280 | tf_op jit(solution)/shard_map/while/body/eval_jaxpr/jit(_take)/gather | solution.py:35
  42.1 1.2 %multiply_convert_fusion = bf16[1,128,2048]{2,1,0:T(8,128)(2,1)} fusion(f32[128]{0:T(128)S(1)} %copy-done.22, f32[2048]{0:T(1024)S(1)} %copy-done.10, f32[128]{0:T(128)S(1)} %add_rsqrt_fusion, f32[1,128,2048]{2,1,0:T(8,128)S(1)} %copy.134, bf16[1,128,2048]{2,1,0:T(8,128)(2,1)S(1)} %copy-done.3), kind=kLoop, calls=%fused_computation.41 | loop fusion | flops 2621440 | bytes 2106368 | tf_op jit(solution)/shard_map/convert_element_type | solution.py:122
  43.3 1.7 %fusion = f32[32,128,64]{1,2,0:T(8,128)S(1)} fusion(bf16[128,32,64]{0,2,1:T(8,128)(2,1)S(1)} %bitcast.136, bf16[32,128,128]{2,1,0:T(8,128)(2,1)S(1)} %copy-done.4, f32[128,32]{0,1:T(8,128)S(1)} %copy-done.17, pred[32]{0:T(512)(128)(4,1)S(1)} %copy-done.27), kind=kOutput, calls=%fused_computation.4 | convolution fusion | flops 404226048 | bytes 2637856 | tf_op jit(solution)/shard_map/while/body/eval_jaxpr/cjhn,cjhp->cnhp/dot_general | solution.py:46
  45.5 0.7 %reshape.512 = bf16[4,1,512]{2,1,0:T(2,128)(2,1)S(1)} reshape(bf16[4,2,256]{2,1,0:T(2,128)(2,1)} %all-to-all-done) | data formatting | bytes 8192
  46.2 0.7 %gather_fusion.1 = bf16[32,4,128]{2,1,0:T(4,128)(2,1)S(1)} fusion(bf16[4,4,128]{2,0,1:T(4,128)(2,1)S(1)} %bitcast.139, s32[1024]{0:T(1024)} %pad_clamp_fusion.1), kind=kCustom, calls=%fused_computation.3 | custom fusion | bytes 65664 | tf_op jit(solution)/shard_map/jit(_take)/gather | solution.py:80
  48.8 5.1 %all-to-all-start.1 = ((bf16[4,2,1024]{2,1,0:T(2,128)(2,1)}), bf16[4,2,1024]{2,1,0:T(2,128)(2,1)S(1)}, u32[]{:S(2)}, u32[]{:S(2)}) async-start(bf16[4,2,1024]{2,1,0:T(2,128)(2,1)} %reshape.513), calls=%async_computation.1 | async-start | bytes 32768 | tf_op jit(solution)/shard_map/all_to_all | solution.py:132
  54.0 1.0 %copy.145 = bf16[1,128,2048]{2,1,0:T(8,128)(2,1)} copy(bf16[1,128,2048]{1,2,0:T(8,128)(2,1)S(1)} %fusion.26) | data formatting | bytes 1048576
  55.4 4.0 %all-to-all-done.1 = bf16[4,2,1024]{2,1,0:T(2,128)(2,1)S(1)} async-done(((bf16[4,2,1024]{2,1,0:T(2,128)(2,1)}), bf16[4,2,1024]{2,1,0:T(2,128)(2,1)S(1)}, u32[]{:S(2)}, u32[]{:S(2)}) %all-to-all-start.1) | async-done | bytes 16416 | tf_op jit(solution)/shard_map/all_to_all | solution.py:132
  59.7 5.6 %psum.7 = f32[1,4]{1,0:T(1,128)S(1)} all-reduce(f32[1,4]{1,0:T(1,128)S(1)} %bitcast.142), channel_id=1, replica_groups=mesh['rep'=2,'sample'=4,'head'=4] {'head'}, use_global_device_ids=true, to_apply=%region_4.6 | all-reduce | flops 4 | bytes 32 | tf_op jit(solution)/shard_map/psum | solution.py:149
  (110 shorter events, 12.3 us)
Async XLA Ops:
  0.6 16.5 %copy-start.2 = (bf16[1,128,2048]{2,1,0:T(8,128)(2,1)S(1)}, bf16[1,128,2048]{2,1,0:T(8,128)(2,1)}, u32[]{:S(2)}) copy-start(bf16[1,128,2048]{2,1,0:T(8,128)(2,1)} %param.18) | copy-start | bytes 1572868
  0.6 17.7 %copy-start.7 = (bf16[1,128,512]{2,1,0:T(8,128)(2,1)S(1)}, bf16[1,128,512]{2,1,0:T(8,128)(2,1)}, u32[]{:S(2)}) copy-start(bf16[1,128,512]{2,1,0:T(8,128)(2,1)} %param.20) | copy-start | bytes 393220
  1.9 17.8 %copy-start.14 = (bf16[1,4,512]{2,1,0:T(4,128)(2,1)S(1)}, bf16[1,4,512]{2,1,0:T(4,128)(2,1)}, u32[]{:S(2)}) copy-start(bf16[1,4,512]{2,1,0:T(4,128)(2,1)} %param.32) | copy-start | bytes 12292
  3.1 42.3 %all-to-all-start = ((bf16[4,2,256]{2,1,0:T(2,128)(2,1)}), bf16[4,2,256]{2,1,0:T(2,128)(2,1)}, u32[]{:S(2)}, u32[]{:S(2)}) async-start(bf16[4,2,256]{2,1,0:T(2,128)(2,1)} %reshape.511), calls=%async_computation | async-start | bytes 8192 | tf_op jit(solution)/shard_map/all_to_all | solution.py:128
  10.1 12.6 %copy-start.21 = (f32[128]{0:T(128)}, f32[128]{0:T(128)S(1)}, u32[]{:S(2)}) copy-start(f32[128]{0:T(128)S(1)} %compare_convert_fusion) | copy-start | bytes 1540
  12.5 9.9 %copy-start.5 = (f32[1,128,2048]{2,1,0:T(8,128)S(1)}, f32[1,128,2048]{2,1,0:T(8,128)}, u32[]{:S(2)}) copy-start(f32[1,128,2048]{2,1,0:T(8,128)} %param.24) | copy-start | bytes 3145732
  17.1 5.6 %copy-start.9 = (f32[1,128,32]{1,2,0:T(8,128)S(1)}, f32[1,128,32]{1,2,0:T(8,128)}, u32[]{:S(2)}) copy-start(f32[1,128,32]{1,2,0:T(8,128)} %param.22) | copy-start | bytes 49156
  17.1 5.6 %copy-start.19 = (f32[32]{0:T(128)S(1)}, f32[32]{0:T(128)}, u32[]{:S(2)}) copy-start(f32[32]{0:T(128)} %param.26) | copy-start | bytes 388
  26.5 4.0 %copy-start = (bf16[32,128,128]{2,1,0:T(8,128)(2,1)S(1)}, bf16[32,128,128]{2,1,0:T(8,128)(2,1)}, u32[]{:S(2)}) copy-start(bf16[32,128,128]{2,1,0:T(8,128)(2,1)} %gather_fusion.2) | copy-start | bytes 3145732
  26.5 4.0 %copy-start.1 = (f32[1,128,2048]{1,2,0:T(8,128)S(1)}, f32[1,128,2048]{1,2,0:T(8,128)}, u32[]{:S(2)}) copy-start(f32[1,128,2048]{1,2,0:T(8,128)} %copy.133) | copy-start | bytes 3145732
  26.5 4.0 %copy-start.26 = (f32[32]{0:T(128)S(1)}, f32[32]{0:T(128)}, u32[]{:S(2)}) copy-start(f32[32]{0:T(128)} %param.27) | copy-start | bytes 388
  32.7 7.0 %copy-start.8 = (bf16[1,128,512]{1,2,0:T(8,128)(2,1)S(1)}, bf16[1,128,512]{1,2,0:T(8,128)(2,1)}, u32[]{:S(2)}) copy-start(bf16[1,128,512]{1,2,0:T(8,128)(2,1)} %copy.136) | copy-start | bytes 393220
  33.1 8.8 %copy-start.28 = (f32[32]{0:T(128)S(1)}, f32[32]{0:T(128)}, u32[]{:S(2)}) copy-start(f32[32]{0:T(128)} %fusion.59) | copy-start | bytes 388
  33.1 8.9 %copy-start.23 = (bf16[1,4,512]{2,1,0:T(4,128)(2,1)S(1)}, bf16[1,4,512]{2,1,0:T(4,128)(2,1)}, u32[]{:S(2)}) copy-start(bf16[1,4,512]{2,1,0:T(4,128)(2,1)} %param.31) | copy-start | bytes 12292
  33.1 8.9 %copy-start.20 = (f32[32]{0:T(128)S(1)}, f32[32]{0:T(128)}, u32[]{:S(2)}) copy-start(f32[32]{0:T(128)} %param.26) | copy-start | bytes 388
  33.1 8.9 %copy-start.24 = (f32[32]{0:T(128)S(1)}, f32[32]{0:T(128)}, u32[]{:S(2)}) copy-start(f32[32]{0:T(128)} %param.25) | copy-start | bytes 388
  33.1 8.9 %copy-start.25 = (f32[1,4,32]{2,1,0:T(4,128)S(1)}, f32[1,4,32]{2,1,0:T(4,128)}, u32[]{:S(2)}) copy-start(f32[1,4,32]{2,1,0:T(4,128)} %param.33) | copy-start | bytes 1540
  33.1 8.9 %copy-start.3 = (bf16[1,128,2048]{2,1,0:T(8,128)(2,1)S(1)}, bf16[1,128,2048]{2,1,0:T(8,128)(2,1)}, u32[]{:S(2)}) copy-start(bf16[1,128,2048]{2,1,0:T(8,128)(2,1)} %param.19) | copy-start | bytes 1572868
  33.1 8.9 %copy-start.10 = (f32[2048]{0:T(1024)S(1)}, f32[2048]{0:T(1024)}, u32[]{:S(2)}) copy-start(f32[2048]{0:T(1024)} %param.28) | copy-start | bytes 24580
  33.2 8.9 %copy-start.22 = (f32[128]{0:T(128)S(1)}, f32[128]{0:T(128)}, u32[]{:S(2)}) copy-start(f32[128]{0:T(128)} %copy-done.21) | copy-start | bytes 1540
  45.0 8.9 %copy-start.29 = (s32[32]{0:T(128)S(1)}, s32[32]{0:T(128)}, u32[]{:S(2)}) copy-start(s32[32]{0:T(128)} %get-tuple-element.77) | copy-start | bytes 388
  45.0 14.5 %copy-start.11 = (bf16[1,4,2048]{2,1,0:T(4,128)(2,1)S(1)}, bf16[1,4,2048]{2,1,0:T(4,128)(2,1)}, u32[]{:S(2)}) copy-start(bf16[1,4,2048]{2,1,0:T(4,128)(2,1)} %param.30) | copy-start | bytes 49156
  45.0 14.5 %copy-start.12 = (bf16[1,4,2048]{2,1,0:T(4,128)(2,1)S(1)}, bf16[1,4,2048]{2,1,0:T(4,128)(2,1)}, u32[]{:S(2)}) copy-start(bf16[1,4,2048]{2,1,0:T(4,128)(2,1)} %param.29) | copy-start | bytes 49156
  48.8 10.7 %all-to-all-start.1 = ((bf16[4,2,1024]{2,1,0:T(2,128)(2,1)}), bf16[4,2,1024]{2,1,0:T(2,128)(2,1)S(1)}, u32[]{:S(2)}, u32[]{:S(2)}) async-start(bf16[4,2,1024]{2,1,0:T(2,128)(2,1)} %reshape.513), calls=%async_computation.1 | async-start | bytes 32768 | tf_op jit(solution)/shard_map/all_to_all | solution.py:132
  (8 other events, 18.0 us)
